TPU v7x, 32 devices: a whole 2x2x4 slice. The times are simulated.
32 devices in a mesh: groups: 2 (over x), frames: 16 (over z, y, core).
Axes of the slice: x: 2, y: 2, z: 4, core: 2. Of those that a mesh axis runs over, the one named last changes fastest.
Arguments:
- features: bfloat16 [4096, 1024], P(('groups', 'frames')), parts along dimension 0, may hold values from -6 to 6
- valid_length: int32 [2], P('groups'), parts along dimension 0, may hold values from 1024 to 2048
- ln1_gain: float32 [1024], replicated, may hold values from 0.5 to 1.5
- w_qkv: bfloat16 [1024, 1536], P('frames'), may hold values from -3 to 3
- w_out: bfloat16 [512, 1024], P('frames'), may hold values from -0.25 to 0.25
- ln2_gain: float32 [1024], replicated, may hold values from 0.5 to 1.5
- w_pw1: bfloat16 [1024, 2048], P('frames'), may hold values from -0.1875 to 0.1875
- w_dw: float32 [9, 1024], replicated, may hold values from -2 to 2
- bn_scale: float32 [1024], replicated, may hold values from 0.5 to 2
- bn_shift: float32 [1024], replicated, may hold values from -3 to 3
- w_pw2: bfloat16 [1024, 1024], P('frames'), may hold values from -0.1875 to 0.1875
Outputs:
- block_out: bfloat16 [4096, 1024], P(('groups', 'frames')), parts along dimension 0
There are 2 independent parts, one for each index of `groups`. A program takes and returns all parts, laid end to end along the dimension named above; an argument that names none is the same for every part. Nothing has to cross between parts.
All inputs are finite; a program needn't handle non-finite values.
Results may differ from a plain program's by a relative error of at most 0.0098.
Values may be sent and summed in bfloat16 or wider, within the bound.
No kernel may reach another device: no remote copies, remote signals or barrier semaphores. Data moves between devices by JAX's collectives and lax.ppermute only.
A program may use at most 128 MiB of HBM per device.

v0:
```python
import math
import jax
import jax.numpy as jnp
from jax import lax
from jax.sharding import PartitionSpec as P

HEADS = 4
HD = 128
EPSILON = 1e-05


def extended(cells, sides, width):
    for axis, dim in sides:
        count = lax.axis_size(axis)
        ends = count - 1
        head = lax.slice_in_dim(cells, 0, width, axis=dim)
        tail = lax.slice_in_dim(cells, cells.shape[dim] - width, cells.shape[dim], axis=dim)
        cells = jnp.concatenate(
            [
                lax.ppermute(tail, axis, [(i, (i + 1) % count) for i in range(ends)]),
                cells,
                lax.ppermute(head, axis, [((i + 1) % count, i) for i in range(ends)]),
            ],
            axis=dim,
        )
    return cells


def layer_norm(values, gain):
    values = values.astype(jnp.float32)
    mean = jnp.mean(values, axis=-1, keepdims=True)
    centred = values - mean
    variance = jnp.mean(centred * centred, axis=-1, keepdims=True)
    return (centred * lax.rsqrt(variance + EPSILON) * gain).astype(jnp.bfloat16)


def per_device(
    features, valid_length, ln1_gain, w_qkv, w_out, ln2_gain, w_pw1, w_dw, bn_scale, bn_shift, w_pw2
):
    limit = valid_length[0]
    local_rows = features.shape[0]
    width = features.shape[1]
    att_width = w_qkv.shape[1] // 3
    scale = 1.0 / math.sqrt(HD)
    tails = (
        lax.all_gather(w_out, "frames", axis=0, tiled=True),
        lax.all_gather(w_pw1, "frames", axis=0, tiled=True),
        lax.all_gather(w_pw2, "frames", axis=0, tiled=True),
    )
    full_out, full_pw1, full_pw2 = tails
    normed1 = layer_norm(features, ln1_gain)
    qkv = jnp.dot(
        normed1,
        lax.all_gather(w_qkv, "frames", axis=0, tiled=True),
        preferred_element_type=jnp.float32,
    ).astype(jnp.bfloat16)
    query_heads = qkv[:, :att_width].reshape(local_rows, HEADS, HD)
    keys = qkv[:, att_width : 2 * att_width]
    values = qkv[:, 2 * att_width :]
    maxima = jnp.full((HEADS, local_rows), -1e30, jnp.float32)
    key_rows = lax.all_gather(keys, "frames", axis=0, tiled=True)
    value_rows = lax.all_gather(values, "frames", axis=0, tiled=True)
    count = key_rows.shape[0]
    key_heads = key_rows.reshape(count, HEADS, HD)
    value_heads = value_rows.reshape(count, HEADS, HD)
    scores = (
        jnp.einsum("qhd,khd->hqk", query_heads, key_heads, preferred_element_type=jnp.float32)
        * scale
    )
    position = jnp.arange(count, dtype=jnp.int32)
    valid = (position < limit)[None, None, :]
    scores = jnp.where(valid, scores, -1e30)
    fresh = jnp.maximum(maxima, jnp.max(scores, axis=-1))
    weights = jnp.where(valid, jnp.exp(scores - fresh[..., None]), 0.0)
    totals = jnp.sum(weights, axis=-1)
    update = jnp.einsum(
        "hqk,khd->hqd",
        weights.astype(jnp.bfloat16),
        value_heads,
        preferred_element_type=jnp.float32,
    )
    summed = update
    maxima, totals, summed = (fresh, totals, summed)
    context = (
        (summed / totals[..., None])
        .transpose(1, 0, 2)
        .reshape(local_rows, att_width)
        .astype(jnp.bfloat16)
    )
    attended = features.astype(jnp.float32) + jnp.dot(
        context, full_out, preferred_element_type=jnp.float32
    )
    normed2 = layer_norm(attended, ln2_gain)
    both = jnp.dot(normed2, full_pw1, preferred_element_type=jnp.float32)
    frame_index = lax.axis_index("frames") * local_rows + jnp.arange(local_rows, dtype=jnp.int32)
    frame_valid = (frame_index < limit)[:, None]
    gated = jnp.where(frame_valid, both[:, :width] * jax.nn.sigmoid(both[:, width:]), 0.0).astype(
        jnp.bfloat16
    )
    half_window = (w_dw.shape[0] - 1) // 2
    widened = extended(gated, (("frames", 0),), half_window)
    widened = widened.astype(jnp.float32)
    conv = jnp.zeros((local_rows, width), jnp.float32)
    for tap in range(w_dw.shape[0]):
        conv = conv + w_dw[tap][None, :] * widened[tap : tap + local_rows]
    activated = jax.nn.silu(bn_scale * conv + bn_shift).astype(jnp.bfloat16)
    result = attended + jnp.dot(activated, full_pw2, preferred_element_type=jnp.float32)
    return result.astype(jnp.bfloat16)


def solution(mesh):
    placed = (
        P(("groups", "frames"), None),
        P("groups"),
        P(),
        P("frames", None),
        P("frames", None),
        P(),
        P("frames", None),
        P(),
        P(),
        P(),
        P("frames", None),
    )
    return jax.shard_map(
        per_device,
        mesh=mesh,
        in_specs=placed,
        out_specs=P(("groups", "frames"), None),
        check_vma=False,
    )
```

profile of v0, /device:TPU:0, one launch (start us, length us, event | category | flops | bytes accessed | tf_op | source)
XLA Modules:
  0.0 286.1 jit_solution(17644636704648669902)
XLA Ops:
  6.5 0.7 all-gather.7.cloned.1.call-update
  7.3 0.0 all-gather.11.cloned.1.call-start
  7.3 1.1 convert_reduce_fusion
  8.4 1.2 fusion.21
  9.6 48.0 %all-gather.7.cloned.1.call-done = bf16[1024,1536]{1,0:T(8,128)(2,1)} async-done(((bf16[64,1536]{1,0:T(8,128)(2,1)}), bf16[1024,1536]{1,0:T(8,128)(2,1)}) %all-gather.7.cloned.1.call-update) | async-done | bytes 3145744 | tf_op jit(solution)/shard_map/all_gather | solution.py:54
  57.6 2.6 convolution_convert_fusion
  60.2 0.7 slice_bitcast_fusion
  61.0 0.0 all-gather.9.cloned.1.call-start
  61.0 0.7 all-gather.9.cloned.1.call-update
  61.7 0.0 all-gather.13.cloned.1.call-start
  61.7 0.5 all-gather.13.cloned.1.call-update
  62.3 0.5 all-gather.15.cloned.1.call-update
  62.9 0.0 all-gather.17.cloned.1.call-start
  62.9 0.5 all-gather.17.cloned.1.call-update
  64.1 37.2 %all-gather.11.cloned.1.call-done = bf16[2048,512]{1,0:T(8,128)(2,1)} async-done(((bf16[128,512]{1,0:T(8,128)(2,1)}), bf16[2048,512]{1,0:T(8,128)(2,1)}) %all-gather.11.cloned.1.call-update) | async-done | bytes 2097168 | tf_op jit(solution)/shard_map/all_gather | solution.py:62
  101.3 2.9 %copy.15 = bf16[2048,512]{0,1:T(8,128)(2,1)S(1)} copy(bf16[2048,512]{1,0:T(8,128)(2,1)} %all-gather.11.cloned.1.call-done) | data formatting | bytes 4194304 | tf_op jit(solution)/shard_map/reshape | solution.py:65
  104.3 39.4 %all-gather.9.cloned.1.call-done = bf16[2048,512]{1,0:T(8,128)(2,1)} async-done(((bf16[128,512]{1,0:T(8,128)(2,1)}), bf16[2048,512]{1,0:T(8,128)(2,1)}) %all-gather.9.cloned.1.call-update) | async-done | bytes 2097168 | tf_op jit(solution)/shard_map/all_gather | solution.py:61
  143.7 2.5 fusion
  146.2 1.1 fusion.1
  147.3 1.3 fusion.16
  148.6 33.8 %all-gather.13.cloned.1.call-done = bf16[512,1024]{1,0:T(8,128)(2,1)} async-done(((bf16[32,1024]{1,0:T(8,128)(2,1)}), bf16[512,1024]{1,0:T(8,128)(2,1)}) %all-gather.13.cloned.1.call-update) | async-done | bytes 1048592 | tf_op jit(solution)/shard_map/all_gather | solution.py:46
  182.5 1.6 fusion.68
  184.1 0.2 multiply_reduce_fusion
  184.4 49.6 %all-gather.15.cloned.1.call-done = bf16[1024,2048]{1,0:T(8,128)(2,1)} async-done(((bf16[64,2048]{1,0:T(8,128)(2,1)}), bf16[1024,2048]{1,0:T(8,128)(2,1)}) %all-gather.15.cloned.1.call-update) | async-done | bytes 4194320 | tf_op jit(solution)/shard_map/all_gather | solution.py:47
  234.0 3.0 %fusion.40 = f32[128,2048]{1,0:T(8,128)S(1)} fusion(bf16[1024,2048]{1,0:T(8,128)(2,1)} %all-gather.15.cloned.1.call-done, f32[128,1024]{1,0:T(8,128)S(1)} %get-tuple-element.22, f32[1024]{0:T(1024)S(1)} %copy-done.2, f32[128]{0:T(128)S(1)} %add_rsqrt_fusion, f32[128]{0:T(128)S(1)} %broadcast_multiply_fusion), kind=kOutput, calls=%fused_computation.54 | convolution fusion | flops 537395200 | bytes 5772288 | tf_op jit(solution)/shard_map/dot_general | solution.py:94
  236.9 0.2 fusion.39
  237.1 2.2 collective-permute-start
  239.3 1.3 collective-permute-start.1
  240.7 1.7 collective-permute-done.1
  242.4 0.1 maximum_convert_fusion
  242.4 33.5 %all-gather.17.cloned.1.call-done = bf16[1024,1024]{1,0:T(8,128)(2,1)} async-done(((bf16[64,1024]{1,0:T(8,128)(2,1)}), bf16[1024,1024]{1,0:T(8,128)(2,1)}) %all-gather.17.cloned.1.call-update) | async-done | bytes 2097168 | tf_op jit(solution)/shard_map/all_gather | solution.py:48
  275.9 3.3 %fusion.9 = bf16[128,1024]{1,0:T(8,128)(2,1)} fusion(f32[128,1024]{1,0:T(8,128)S(1)} %get-tuple-element.22, bf16[1024,1024]{1,0:T(8,128)(2,1)} %all-gather.17.cloned.1.call-done, f32[136,1024]{1,0:T(8,128)S(1)} %maximum_convert_fusion, f32[1024]{0:T(1024)S(1)} %copy-done.3, f32[1024]{0:T(1024)S(1)} %bitcast.52, f32[1024]{0:T(1024)S(1)} %bitcast.53, ...), kind=kOutput, calls=%fused_computation.13 | convolution fusion | flops 271843328 | bytes 7647232 | tf_op jit(solution)/shard_map/dot_general | solution.py:107
  (23 shorter events, 0.2 us)
Async XLA Ops:
  6.5 51.0 %all-gather.7.cloned.1.call-start = ((), (), s32[]{:S(2)}) async-start(), calls=%async_computation | async-start | bytes 3342336 | tf_op jit(solution)/shard_map/all_gather | solution.py:54
  7.3 94.1 %all-gather.11.cloned.1.call-start = ((), (), s32[]{:S(2)}) async-start(), calls=%async_computation.2 | async-start | bytes 2228224 | tf_op jit(solution)/shard_map/all_gather | solution.py:62
  61.0 82.7 %all-gather.9.cloned.1.call-start = ((), (), s32[]{:S(2)}) async-start(), calls=%async_computation.1 | async-start | bytes 2228224 | tf_op jit(solution)/shard_map/all_gather | solution.py:61
  61.7 120.8 %all-gather.13.cloned.1.call-start = ((), (), s32[]{:S(2)}) async-start(), calls=%async_computation.3 | async-start | bytes 1114112 | tf_op jit(solution)/shard_map/all_gather | solution.py:46
  62.3 171.7 %all-gather.15.cloned.1.call-start = ((), (), s32[]{:S(2)}) async-start(), calls=%async_computation.4 | async-start | bytes 4456448 | tf_op jit(solution)/shard_map/all_gather | solution.py:47
  62.9 213.1 %all-gather.17.cloned.1.call-start = ((), (), s32[]{:S(2)}) async-start(), calls=%async_computation.5 | async-start | bytes 2228224 | tf_op jit(solution)/shard_map/all_gather | solution.py:48
  147.3 35.2 %copy-start = (bf16[128,1024]{1,0:T(8,128)(2,1)S(1)}, bf16[128,1024]{1,0:T(8,128)(2,1)}, u32[]{:S(2)}) copy-start(bf16[128,1024]{1,0:T(8,128)(2,1)} %param.11) | copy-start | bytes 786436
  147.3 86.7 %copy-start.2 = (f32[1024]{0:T(1024)S(1)}, f32[1024]{0:T(1024)}, u32[]{:S(2)}) copy-start(f32[1024]{0:T(1024)} %param.16) | copy-start | bytes 12292
  184.1 56.5 %copy-start.1 = (f32[9,1024]{1,0:T(8,128)S(1)}, f32[9,1024]{1,0:T(8,128)}, u32[]{:S(2)}) copy-start(f32[9,1024]{1,0:T(8,128)} %param.18) | copy-start | bytes 110596
  184.1 91.8 %copy-start.3 = (f32[1024]{0:T(1024)S(1)}, f32[1024]{0:T(1024)}, u32[]{:S(2)}) copy-start(f32[1024]{0:T(1024)} %param.20) | copy-start | bytes 12292
  184.1 91.8 %copy-start.4 = (f32[1024]{0:T(1024)S(1)}, f32[1024]{0:T(1024)}, u32[]{:S(2)}) copy-start(f32[1024]{0:T(1024)} %param.19) | copy-start | bytes 12292
  237.1 3.5 %collective-permute-start = (bf16[4,1024]{1,0:T(4,128)(2,1)S(1)}, bf16[4,1024]{1,0:T(4,128)(2,1)S(1)}, u32[]{:S(2)}, u32[]{:S(2)}) collective-permute-start(bf16[4,1024]{1,0:T(4,128)(2,1)S(1)} %get-tuple-element.8), channel_id=1, source_target_pairs={{0,1},{1,2},{2,3},{3,4},{4,5},{5,6},{6,7},{7,8},{8,9},{9,10},{10,1... | collective-permute-start | bytes 24584 | tf_op jit(solution)/shard_map/ppermute | solution.py:20
  239.3 3.1 %collective-permute-start.1 = (bf16[4,1024]{1,0:T(4,128)(2,1)S(1)}, bf16[4,1024]{1,0:T(4,128)(2,1)S(1)}, u32[]{:S(2)}, u32[]{:S(2)}) collective-permute-start(bf16[4,1024]{1,0:T(4,128)(2,1)S(1)} %get-tuple-element.9), channel_id=1, source_target_pairs={{1,0},{2,1},{3,2},{4,3},{5,4},{6,5},{7,6},{8,7},{9,8},{10,9},{11,1... | collective-permute-start | bytes 24584 | tf_op jit(solution)/shard_map/ppermute | solution.py:22
Sparse Core Ops, SparseCore 0:
  9.6 47.8 all-gather.6
  61.1 40.1 all-gather.10
  103.5 40.1 all-gather.8
  145.7 36.7 all-gather.12
  184.5 49.4 all-gather.14
  236.0 39.8 all-gather.16
where the time goes:
time: 287 us; the launch traced here: 286 us
  waiting for transfers between devices  246 us (86%)
  matrix products  14.4 us (5%)
  between operations  14.3 us (5%)
  other arithmetic  3.81 us (1%)
  local copies, waits for them, and re-layouts  3.71 us (1%)
  starting transfers between devices  3.65 us (1%)
    all_gather x1, waiting for transfers between devices, per_device(): lax.all_gather(w_pw1, 'frames', axis=0, tiled=True)  49.6 us
    all_gather x1, waiting for transfers between devices, per_device(): lax.all_gather(w_qkv, 'frames', axis=0, tiled=True)  48 us
    all_gather x1, waiting for transfers between devices, per_device(): key_rows = lax.all_gather(keys, 'frames', axis=0, tiled=True)  39.4 us
    all_gather x1, waiting for transfers between devices, per_device(): value_rows = lax.all_gather(values, 'frames', axis=0, tiled=True)  37.2 us
    all_gather x1, waiting for transfers between devices, per_device(): lax.all_gather(w_out, 'frames', axis=0, tiled=True)  33.8 us
    all_gather x1, waiting for transfers between devices, per_device(): lax.all_gather(w_pw2, 'frames', axis=0, tiled=True)  33.5 us
  transfers between devices with their start and end apart: 8, of which 7 were waited for; matrix products, arithmetic and copies ran while one was open for 5% of the time, Pallas kernels for 0%

commit v1 on v0

--- a/solution.py
+++ b/solution.py
@@ -58,8 +58,15 @@
     keys = qkv[:, att_width : 2 * att_width]
     values = qkv[:, 2 * att_width :]
     maxima = jnp.full((HEADS, local_rows), -1e30, jnp.float32)
-    key_rows = lax.all_gather(keys, "frames", axis=0, tiled=True)
-    value_rows = lax.all_gather(values, "frames", axis=0, tiled=True)
+
+    def scenes_load(view, vals, bus_axis):
+        return jnp.split(
+            jax.lax.all_gather(jnp.concatenate([view, vals], 1), bus_axis, axis=0, tiled=True),
+            [view.shape[1]],
+            axis=1,
+        )
+
+    key_rows, value_rows = scenes_load(keys, values, "frames")
     count = key_rows.shape[0]
     key_heads = key_rows.reshape(count, HEADS, HD)
     value_heads = value_rows.reshape(count, HEADS, HD)

time: 287 us -> 253 us (0.88)
  waiting for transfers between devices: 246 us -> 208 us
  local copies, waits for them, and re-layouts: 3.71 us -> 7.28 us
    all_gather x2 -> x1, waiting for transfers between devices: 76.6 us -> 46.9 us  [scenes_load(): jax.lax.all_gather(jnp.concatenate([view, vals], 1), bus_axis, axis=0, ti...]
    all_gather x1, waiting for transfers between devices: 33.8 us -> 27.1 us  [per_device(): lax.all_gather(w_out, 'frames', axis=0, tiled=True)]
    unnamed x11 -> x13, local copies, waits for them, and re-layouts: 0.74 us -> 4.04 us
  transfers between devices with their start and end apart: 8 -> 7, of which waited for: 7 -> 6; matrix products, arithmetic and copies ran while one was open for 5% -> 7% of each run, Pallas kernels for 0% -> 0%
where the time goes in v1:
time: 253 us; the launch traced here: 252 us
  waiting for transfers between devices  208 us (82%)
  matrix products  14.5 us (6%)
  between operations  14 us (6%)
  local copies, waits for them, and re-layouts  7.28 us (3%)
  starting transfers between devices  4.48 us (2%)
  other arithmetic  3.81 us (2%)
    all_gather x1, waiting for transfers between devices, per_device(): lax.all_gather(w_pw1, 'frames', axis=0, tiled=True)  49.6 us
    all_gather x1, waiting for transfers between devices, per_device(): lax.all_gather(w_qkv, 'frames', axis=0, tiled=True)  48 us
    all_gather x1, waiting for transfers between devices, scenes_load(): jax.lax.all_gather(jnp.concatenate([view, vals], 1), bus_axis, axis=0, ti...  46.9 us
    all_gather x1, waiting for transfers between devices, per_device(): lax.all_gather(w_pw2, 'frames', axis=0, tiled=True)  33.5 us
    all_gather x1, waiting for transfers between devices, per_device(): lax.all_gather(w_out, 'frames', axis=0, tiled=True)  27.1 us
  transfers between devices with their start and end apart: 7, of which 6 were waited for; matrix products, arithmetic and copies ran while one was open for 7% of the time, Pallas kernels for 0%

profile of v1, /device:TPU:0, one launch (start us, length us, event | category | flops | bytes accessed | tf_op | source)
XLA Modules:
  0.0 252.4 jit_solution(2929440256516899960)
XLA Ops:
  6.5 0.7 all-gather.6.cloned.1.call-update
  7.3 0.0 all-gather.8.cloned.1.call-start
  7.3 1.1 convert_reduce_fusion
  8.4 1.2 fusion.21
  9.6 48.0 %all-gather.6.cloned.1.call-done = bf16[1024,1536]{1,0:T(8,128)(2,1)} async-done(((bf16[64,1536]{1,0:T(8,128)(2,1)}), bf16[1024,1536]{1,0:T(8,128)(2,1)}) %all-gather.6.cloned.1.call-update) | async-done | bytes 3145744 | tf_op jit(solution)/shard_map/all_gather | solution.py:54
  57.6 2.6 %convolution_convert_fusion = bf16[128,1536]{1,0:T(8,128)(2,1)S(1)} fusion(bf16[1024,1536]{1,0:T(8,128)(2,1)} %all-gather.6.cloned.1.call-done, bf16[128,1024]{1,0:T(8,128)(2,1)} %param.11, f32[1024]{0:T(1024)} %param.13, f32[128]{0:T(128)S(1)} %add_rsqrt_fusion.1, f32[128]{0:T(128)S(1)} %broadcast_multiply_fusion.1), kind=kOutput, calls=%fused_computation.5 | convolution fusion | flops 403505152 | bytes 3806208 | tf_op jit(solution)/shard_map/dot_general | solution.py:52
  60.2 0.7 concatenate.8
  61.0 0.0 all-gather.8.cloned.1.call-update
  61.0 0.0 all-gather.10.cloned.1.call-start
  61.0 0.7 all-gather.10.cloned.1.call-update
  61.7 0.0 all-gather.12.cloned.1.call-start
  61.8 0.5 all-gather.12.cloned.1.call-update
  62.3 0.0 all-gather.14.cloned.1.call-start
  62.3 0.5 all-gather.14.cloned.1.call-update
  63.6 46.9 %all-gather.8.cloned.1.call-done = bf16[2048,1024]{1,0:T(8,128)(2,1)} async-done(((bf16[128,1024]{1,0:T(8,128)(2,1)}), bf16[2048,1024]{1,0:T(8,128)(2,1)}) %all-gather.8.cloned.1.call-update) | async-done | bytes 4194320 | tf_op jit(solution)/shard_map/all_gather | solution.py:64
  110.5 4.0 %slice_bitcast_fusion = (bf16[256,4,8,128]{3,2,1,0:T(8,128)(2,1)}, bf16[2048,512]{1,0:T(8,128)(2,1)S(1)}) fusion(bf16[2048,1024]{1,0:T(8,128)(2,1)} %all-gather.8.cloned.1.call-done), kind=kLoop, calls=%fused_computation.9 | loop fusion | bytes 8388608
  114.5 2.5 copy.15
  117.0 2.7 %fusion = (f32[4,128]{1,0:T(4,128)S(1)}, f32[4,128,2048]{2,1,0:T(8,128)S(1)}) fusion(pred[2048]{0:T(1024)(128)(4,1)S(1)} %iota_compare_fusion, bf16[256,4,8,128]{3,2,1,0:T(8,128)(2,1)} %get-tuple-element.5, bf16[128,1536]{1,0:T(8,128)(2,1)S(1)} %convolution_convert_fusion), kind=kOutput, calls=%fused_computation.2 | convolution fusion | flops 271580672 | bytes 6426624 | tf_op jit(solution)/shard_map/qhd,khd->hqk/dot_general | solution.py:74
  119.7 1.1 fusion.1
  120.8 1.3 fusion.16
  122.1 27.1 %all-gather.10.cloned.1.call-done = bf16[512,1024]{1,0:T(8,128)(2,1)} async-done(((bf16[32,1024]{1,0:T(8,128)(2,1)}), bf16[512,1024]{1,0:T(8,128)(2,1)}) %all-gather.10.cloned.1.call-update) | async-done | bytes 1048592 | tf_op jit(solution)/shard_map/all_gather | solution.py:46
  149.2 1.6 fusion.68
  150.8 0.2 multiply_reduce_fusion
  151.0 49.6 %all-gather.12.cloned.1.call-done = bf16[1024,2048]{1,0:T(8,128)(2,1)} async-done(((bf16[64,2048]{1,0:T(8,128)(2,1)}), bf16[1024,2048]{1,0:T(8,128)(2,1)}) %all-gather.12.cloned.1.call-update) | async-done | bytes 4194320 | tf_op jit(solution)/shard_map/all_gather | solution.py:47
  200.7 3.0 %fusion.40 = f32[128,2048]{1,0:T(8,128)S(1)} fusion(bf16[1024,2048]{1,0:T(8,128)(2,1)} %all-gather.12.cloned.1.call-done, f32[128,1024]{1,0:T(8,128)S(1)} %get-tuple-element.21, f32[1024]{0:T(1024)S(1)} %copy-done.3, f32[128]{0:T(128)S(1)} %add_rsqrt_fusion, f32[128]{0:T(128)S(1)} %broadcast_multiply_fusion), kind=kOutput, calls=%fused_computation.55 | convolution fusion | flops 537395200 | bytes 5772288 | tf_op jit(solution)/shard_map/dot_general | solution.py:101
  203.6 0.2 fusion.39
  203.8 1.3 collective-permute-start.1
  205.1 3.0 %collective-permute-start = (bf16[4,1024]{1,0:T(4,128)(2,1)S(1)}, bf16[4,1024]{1,0:T(4,128)(2,1)S(1)}, u32[]{:S(2)}, u32[]{:S(2)}) collective-permute-start(bf16[4,1024]{1,0:T(4,128)(2,1)S(1)} %get-tuple-element.7), channel_id=1, source_target_pairs={{0,1},{1,2},{2,3},{3,4},{4,5},{5,6},{6,7},{7,8},{8,9},{9,10},{10,1... | collective-permute-start | bytes 24584 | tf_op jit(solution)/shard_map/ppermute | solution.py:20
  208.2 0.8 collective-permute-done
  209.0 0.1 maximum_convert_fusion
  209.1 33.5 %all-gather.14.cloned.1.call-done = bf16[1024,1024]{1,0:T(8,128)(2,1)} async-done(((bf16[64,1024]{1,0:T(8,128)(2,1)}), bf16[1024,1024]{1,0:T(8,128)(2,1)}) %all-gather.14.cloned.1.call-update) | async-done | bytes 2097168 | tf_op jit(solution)/shard_map/all_gather | solution.py:48
  242.6 3.3 %fusion.9 = bf16[128,1024]{1,0:T(8,128)(2,1)} fusion(f32[128,1024]{1,0:T(8,128)S(1)} %get-tuple-element.21, bf16[1024,1024]{1,0:T(8,128)(2,1)} %all-gather.14.cloned.1.call-done, f32[136,1024]{1,0:T(8,128)S(1)} %maximum_convert_fusion, f32[1024]{0:T(1024)S(1)} %copy-done.4, f32[1024]{0:T(1024)S(1)} %bitcast.52, f32[1024]{0:T(1024)S(1)} %bitcast.53, ...), kind=kOutput, calls=%fused_computation.14 | convolution fusion | flops 271843328 | bytes 7647232 | tf_op jit(solution)/shard_map/dot_general | solution.py:114
  (23 shorter events, 0.1 us)
Async XLA Ops:
  6.5 51.0 %all-gather.6.cloned.1.call-start = ((), (), s32[]{:S(2)}) async-start(), calls=%async_computation | async-start | bytes 3342336 | tf_op jit(solution)/shard_map/all_gather | solution.py:54
  7.3 103.2 %all-gather.8.cloned.1.call-start = ((), (), s32[]{:S(2)}) async-start(), calls=%async_computation.1 | async-start | bytes 4456448 | tf_op jit(solution)/shard_map/all_gather | solution.py:64
  61.0 88.2 %all-gather.10.cloned.1.call-start = ((), (), s32[]{:S(2)}) async-start(), calls=%async_computation.2 | async-start | bytes 1114112 | tf_op jit(solution)/shard_map/all_gather | solution.py:46
  61.7 139.0 %all-gather.12.cloned.1.call-start = ((), (), s32[]{:S(2)}) async-start(), calls=%async_computation.3 | async-start | bytes 4456448 | tf_op jit(solution)/shard_map/all_gather | solution.py:47
  62.3 180.3 %all-gather.14.cloned.1.call-start = ((), (), s32[]{:S(2)}) async-start(), calls=%async_computation.4 | async-start | bytes 2228224 | tf_op jit(solution)/shard_map/all_gather | solution.py:48
  117.0 3.8 %copy-start.1 = (bf16[2048,512]{0,1:T(8,128)(2,1)S(1)}, bf16[2048,512]{0,1:T(8,128)(2,1)}, u32[]{:S(2)}) copy-start(bf16[2048,512]{0,1:T(8,128)(2,1)} %copy.15) | copy-start | bytes 6291460
  120.8 28.4 %copy-start = (bf16[128,1024]{1,0:T(8,128)(2,1)S(1)}, bf16[128,1024]{1,0:T(8,128)(2,1)}, u32[]{:S(2)}) copy-start(bf16[128,1024]{1,0:T(8,128)(2,1)} %param.11) | copy-start | bytes 786436
  120.8 79.9 %copy-start.3 = (f32[1024]{0:T(1024)S(1)}, f32[1024]{0:T(1024)}, u32[]{:S(2)}) copy-start(f32[1024]{0:T(1024)} %param.16) | copy-start | bytes 12292
  150.8 57.4 %copy-start.2 = (f32[9,1024]{1,0:T(8,128)S(1)}, f32[9,1024]{1,0:T(8,128)}, u32[]{:S(2)}) copy-start(f32[9,1024]{1,0:T(8,128)} %param.18) | copy-start | bytes 110596
  150.8 91.7 %copy-start.4 = (f32[1024]{0:T(1024)S(1)}, f32[1024]{0:T(1024)}, u32[]{:S(2)}) copy-start(f32[1024]{0:T(1024)} %param.20) | copy-start | bytes 12292
  150.8 91.7 %copy-start.5 = (f32[1024]{0:T(1024)S(1)}, f32[1024]{0:T(1024)}, u32[]{:S(2)}) copy-start(f32[1024]{0:T(1024)} %param.19) | copy-start | bytes 12292
  203.8 4.4 %collective-permute-start.1 = (bf16[4,1024]{1,0:T(4,128)(2,1)S(1)}, bf16[4,1024]{1,0:T(4,128)(2,1)S(1)}, u32[]{:S(2)}, u32[]{:S(2)}) collective-permute-start(bf16[4,1024]{1,0:T(4,128)(2,1)S(1)} %get-tuple-element.8), channel_id=1, source_target_pairs={{1,0},{2,1},{3,2},{4,3},{5,4},{6,5},{7,6},{8,7},{9,8},{10,9},{11,1... | collective-permute-start | bytes 24584 | tf_op jit(solution)/shard_map/ppermute | solution.py:22
  205.1 3.8 %collective-permute-start = (bf16[4,1024]{1,0:T(4,128)(2,1)S(1)}, bf16[4,1024]{1,0:T(4,128)(2,1)S(1)}, u32[]{:S(2)}, u32[]{:S(2)}) collective-permute-start(bf16[4,1024]{1,0:T(4,128)(2,1)S(1)} %get-tuple-element.7), channel_id=1, source_target_pairs={{0,1},{1,2},{2,3},{3,4},{4,5},{5,6},{6,7},{7,8},{8,9},{9,10},{10,1... | collective-permute-start | bytes 24584 | tf_op jit(solution)/shard_map/ppermute | solution.py:20
Sparse Core Ops, SparseCore 0:
  9.6 47.8 all-gather.5
  61.1 49.3 all-gather.7
  112.7 36.4 all-gather.9
  151.2 49.4 all-gather.11
  202.7 39.8 all-gather.13
